TPU v7x, 32 devices: a whole 2x2x4 slice. The times are simulated.
32 devices in a mesh: col: 8 (over y, x, core), dev: 4 (over z).
Axes of the slice: x: 2, y: 2, z: 4, core: 2. Of those that a mesh axis runs over, the one named last changes fastest.
Arguments:
- first_factor: bfloat16 [16, 1024, 2048], P(None, 'col', 'dev'), may hold values from -1 to 1
- second_factor: bfloat16 [16, 1024, 2048], P(None, 'dev', 'col'), may hold values from -1 to 1
- amplitudes: bfloat16 [512, 1024, 1024], P(None, 'col', 'dev'), may hold values from -0.0059814453 to 0.0059814453
Outputs:
- ladder: float32 [512, 256], P(('col', 'dev'))
All inputs are finite; a program needn't handle non-finite values.
Results may differ from a plain program's by a relative error of at most 0.0029.
Values may be sent and summed in bfloat16 or wider, within the bound.
A program may use at most 128 MiB of HBM per device.

v0:
```python
import jax
import jax.numpy as jnp
from jax import lax
from jax.sharding import PartitionSpec as P


def on_device(first_factor, second_factor, amplitudes):
    width_a, block_c, _ = first_factor.shape
    width_b, block_d, _ = second_factor.shape
    pairs = amplitudes.shape[0]
    first_whole = lax.all_gather(first_factor, "dev", axis=2, tiled=True).reshape(
        width_a * block_c, -1
    )
    second_whole = lax.all_gather(second_factor, "col", axis=2, tiled=True).reshape(
        width_b * block_d, -1
    )
    tile_sum = lax.dot_general(
        first_whole, second_whole, (((1,), (1,)), ((), ())), preferred_element_type=jnp.float32
    )
    tile = tile_sum.astype(jnp.bfloat16).reshape(width_a, block_c, width_b, block_d)
    partial_value = jnp.einsum(
        "acbd,pcd->pab", tile, amplitudes, preferred_element_type=jnp.float32
    )
    partial_value = partial_value.reshape(pairs, width_a * width_b)
    halfway = lax.psum_scatter(partial_value, "col", scatter_dimension=0, tiled=True)
    return lax.psum_scatter(halfway, "dev", scatter_dimension=0, tiled=True)


def solution(mesh):
    placed = (P(None, "col", "dev"), P(None, "dev", "col"), P(None, "col", "dev"))
    return jax.shard_map(
        on_device, mesh=mesh, in_specs=placed, out_specs=P(("col", "dev"), None), check_vma=False
    )
```

profile of v0, /device:TPU:0, one launch (start us, length us, event | category | flops | bytes accessed | tf_op | source)
XLA Modules:
  0.0 409.0 jit_solution(3210589852640393744)
XLA Ops:
  6.5 0.0 all-gather.3.cloned.1.call-start
  6.5 0.7 all-gather.3.cloned.1.call-update
  7.3 0.0 all-gather.5.cloned.1.call-start
  7.3 0.7 all-gather.5.cloned.1.call-update
  8.0 0.0 reduce-scatter.3.cloned.1.call-start
  8.1 153.2 %all-gather.3.cloned.1.call-done = bf16[16,128,2048]{2,1,0:T(8,128)(2,1)} async-done(((bf16[16,128,512]{2,1,0:T(8,128)(2,1)}), bf16[16,128,2048]{2,1,0:T(8,128)(2,1)}) %all-gather.3.cloned.1.call-update) | async-done | bytes 8388624 | tf_op jit(solution)/shard_map/all_gather | solution.py:11
  161.3 93.1 %all-gather.5.cloned.1.call-done = bf16[16,256,2048]{2,1,0:T(8,128)(2,1)} async-done(((bf16[16,256,256]{2,1,0:T(8,128)(2,1)}), bf16[16,256,2048]{2,1,0:T(8,128)(2,1)}) %all-gather.5.cloned.1.call-update) | async-done | bytes 16777232 | tf_op jit(solution)/shard_map/all_gather | solution.py:14
  254.4 40.6 %convolution_convert_fusion = bf16[2048,4096]{1,0:T(8,128)(2,1)S(1)} fusion(bf16[2048,2048]{1,0:T(8,128)(2,1)} %bitcast.24, bf16[4096,2048]{1,0:T(8,128)(2,1)} %bitcast.23), kind=kOutput, calls=%fused_computation.4 | convolution fusion | flops 34368126976 | bytes 41943040 | tf_op jit(solution)/shard_map/dot_general | solution.py:17
  295.0 8.7 %copy.7 = bf16[256,8,16,256]{3,2,1,0:T(8,128)(2,1)} copy(bf16[256,8,16,256]{3,1,2,0:T(8,128)(2,1)S(1)} %bitcast.20) | data formatting | bytes 33554432
  303.8 42.0 %fusion = f32[16,16,512,1]{2,1,3,0:T(8,128)S(1)} fusion(bf16[512,128,256]{2,1,0:T(8,128)(2,1)} %param.5, bf16[16,128,16,256]{3,2,1,0:T(8,128)(2,1)} %bitcast.21), kind=kOutput, calls=%fused_computation | convolution fusion | flops 8589934592 | bytes 50855936 | tf_op jit(solution)/shard_map/acbd,pcd->pab/dot_general | solution.py:21
  345.7 1.0 copy.5
  346.7 0.0 reduce-scatter.3.cloned.1.call-update
  346.8 0.0 reduce-scatter.5.cloned.1.call-start
  346.8 34.2 %reduce-scatter.3.cloned.1.call-done = f32[64,256]{1,0:T(8,128)} async-done(((f32[512,256]{1,0:T(8,128)}), f32[64,256]{1,0:T(8,128)}) %reduce-scatter.3.cloned.1.call-update) | async-done | bytes 65552 | tf_op jit(solution)/shard_map/reduce_scatter | solution.py:25
  381.0 0.0 reduce-scatter.5.cloned.1.call-update
  381.1 21.4 %reduce-scatter.5.cloned.1.call-done = f32[16,256]{1,0:T(8,128)} async-done(((f32[64,256]{1,0:T(8,128)}), f32[16,256]{1,0:T(8,128)}) %reduce-scatter.5.cloned.1.call-update) | async-done | bytes 16400 | tf_op jit(solution)/shard_map/reduce_scatter | solution.py:26
Async XLA Ops:
  6.5 154.7 %all-gather.3.cloned.1.call-start = ((), (), s32[]{:S(2)}) async-start(), calls=%async_computation.2 | async-start | bytes 10485760 | tf_op jit(solution)/shard_map/all_gather | solution.py:11
  7.3 247.1 %all-gather.5.cloned.1.call-start = ((), (), s32[]{:S(2)}) async-start(), calls=%async_computation.3 | async-start | bytes 18874368 | tf_op jit(solution)/shard_map/all_gather | solution.py:14
  8.0 373.0 %reduce-scatter.3.cloned.1.call-start = ((), (), s32[]{:S(2)}) async-start(), calls=%async_computation.4 | async-start | bytes 589824 | tf_op jit(solution)/shard_map/reduce_scatter | solution.py:25
  346.8 55.7 %reduce-scatter.5.cloned.1.call-start = ((), (), s32[]{:S(2)}) async-start(), calls=%async_computation.5 | async-start | bytes 81920 | tf_op jit(solution)/shard_map/reduce_scatter | solution.py:26
Sparse Core Ops, SparseCore 0:
  8.9 152.3 all-gather.2
  163.1 91.1 all-gather.4
  346.9 34.1 reduce-scatter.2
  383.1 19.2 reduce-scatter.4
where the time goes:
time: 409 us
  waiting for transfers between devices  303 us (74%)
  matrix products  82.6 us (20%)
  between operations  13.1 us (3%)
  local copies, waits for them, and re-layouts  9.73 us (2%)
    all_gather x1, waiting for transfers between devices, on_device(): lax.all_gather(first_factor, 'dev', axis=2, tiled=True)  153 us
    all_gather x1, waiting for transfers between devices, on_device(): lax.all_gather(second_factor, 'col', axis=2, tiled=True)  93.1 us
    dot_general x1, matrix products, on_device(): jnp.einsum('acbd,pcd->pab', tile, amplitudes, preferred_element_type=jnp....  42 us
    dot_general x1, matrix products, on_device(): lax.dot_general(first_whole, second_whole, (((1,), (1,)), ((), ())), pref...  40.6 us
    reduce_scatter x1, waiting for transfers between devices, on_device(): lax.psum_scatter(partial_value, 'col', scatter_dimension=0, tiled=True)  34.2 us
    reduce_scatter x1, waiting for transfers between devices, on_device(): return lax.psum_scatter(halfway, 'dev', scatter_dimension=0, tiled=True)  21.4 us
    unnamed x1, local copies, waits for them, and re-layouts  8.73 us
  transfers between devices with their start and end apart: 4, of which 4 were waited for; matrix products, arithmetic and copies ran while one was open for 0% of the time, Pallas kernels for 0%

commit v1 on v0

--- a/solution.py
+++ b/solution.py
@@ -2,6 +2,17 @@
 import jax.numpy as jnp
 from jax import lax
 from jax.sharding import PartitionSpec as P
+
+
+def ring_gather(x, axis, dim):
+    ways = lax.axis_size(axis)
+    pieces = [x]
+    for far in range(1, ways):
+        pieces.append(
+            lax.ppermute(pieces[far - 1], axis, [(d, (d - 1) % ways) for d in range(ways)])
+        )
+    line = jnp.concatenate(pieces, axis=dim)
+    return jnp.roll(line, lax.axis_index(axis) * x.shape[dim], axis=dim)
 
 
 def on_device(first_factor, second_factor, amplitudes):
@@ -11,9 +22,7 @@
     first_whole = lax.all_gather(first_factor, "dev", axis=2, tiled=True).reshape(
         width_a * block_c, -1
     )
-    second_whole = lax.all_gather(second_factor, "col", axis=2, tiled=True).reshape(
-        width_b * block_d, -1
-    )
+    second_whole = ring_gather(second_factor, "col", 2).reshape(width_b * block_d, -1)
     tile_sum = lax.dot_general(
         first_whole, second_whole, (((1,), (1,)), ((), ())), preferred_element_type=jnp.float32
     )

time: 409 us -> 393 us (0.961)
  waiting for transfers between devices: 303 us -> 197 us
  local copies, waits for them, and re-layouts: 9.73 us -> 94.5 us
  starting transfers between devices: 0.12 us -> 21.7 us
  matrix products: 82.6 us -> 64.5 us
    all_gather x1, waiting for transfers between devices: 153 us -> 0.01 us  [on_device(): lax.all_gather(first_factor, 'dev', axis=2, tiled=True)]
    ppermute x0 -> x7, waiting for transfers between devices: none -> 142 us  [ring_gather(): lax.ppermute(pieces[far - 1], axis, [(d, (d - 1) % ways) for d in range(w...]
    all_gather x1 -> x0, waiting for transfers between devices: 93.1 us -> none  [on_device(): lax.all_gather(second_factor, 'col', axis=2, tiled=True)]
    unnamed x1 -> x33, local copies, waits for them, and re-layouts: 8.73 us -> 84.7 us
    ppermute x0 -> x7, starting transfers between devices: none -> 21.6 us  [ring_gather(): lax.ppermute(pieces[far - 1], axis, [(d, (d - 1) % ways) for d in range(w...]
    dot_general x1, matrix products: 42 us -> 22.5 us  [on_device(): jnp.einsum('acbd,pcd->pab', tile, amplitudes, preferred_element_type=jnp....]
    dynamic_slice x0 -> x1, local copies, waits for them, and re-layouts: none -> 6.63 us  [ring_gather(): return jnp.roll(line, lax.axis_index(axis) * x.shape[dim], axis=dim)]
  transfers between devices with their start and end apart: 4 -> 10, of which waited for: 4 -> 8; matrix products, arithmetic and copies ran while one was open for 0% -> 20% of each run, Pallas kernels for 0% -> 0%
where the time goes in v1:
time: 393 us; the launch traced here: 391 us
  waiting for transfers between devices  197 us (50%)
  local copies, waits for them, and re-layouts  94.5 us (24%)
  matrix products  64.5 us (16%)
  starting transfers between devices  21.7 us (6%)
  between operations  13.3 us (3%)
    ppermute x7, waiting for transfers between devices, ring_gather(): lax.ppermute(pieces[far - 1], axis, [(d, (d - 1) % ways) for d in range(w...  142 us
    unnamed x33, local copies, waits for them, and re-layouts  84.7 us
    dot_general x1, matrix products, on_device(): lax.dot_general(first_whole, second_whole, (((1,), (1,)), ((), ())), pref...  42 us
    reduce_scatter x1, waiting for transfers between devices, on_device(): lax.psum_scatter(partial_value, 'col', scatter_dimension=0, tiled=True)  33.6 us
    dot_general x1, matrix products, on_device(): jnp.einsum('acbd,pcd->pab', tile, amplitudes, preferred_element_type=jnp....  22.5 us
    ppermute x7, starting transfers between devices, ring_gather(): lax.ppermute(pieces[far - 1], axis, [(d, (d - 1) % ways) for d in range(w...  21.6 us
    reduce_scatter x1, waiting for transfers between devices, on_device(): return lax.psum_scatter(halfway, 'dev', scatter_dimension=0, tiled=True)  21.6 us
  transfers between devices with their start and end apart: 10, of which 8 were waited for; matrix products, arithmetic and copies ran while one was open for 20% of the time, Pallas kernels for 0%

profile of v1, /device:TPU:0, one launch (start us, length us, event | category | flops | bytes accessed | tf_op | source)
XLA Modules:
  0.0 391.1 jit_solution(609703380871732549)
XLA Ops:
  6.5 3.4 collective-permute-start
  9.9 23.9 %collective-permute-done = bf16[16,256,256]{2,1,0:T(8,128)(2,1)S(1)} collective-permute-done((bf16[16,256,256]{2,1,0:T(8,128)(2,1)}, bf16[16,256,256]{2,1,0:T(8,128)(2,1)S(1)}, u32[]{:S(2)}, u32[]{:S(2)}) %collective-permute-start) | collective-permute-done | bytes 2097184 | tf_op jit(solution)/shard_map/ppermute | solution.py:12
  35.1 2.7 collective-permute-start.1
  37.8 23.6 %collective-permute-done.1 = bf16[16,256,256]{2,1,0:T(8,128)(2,1)S(1)} collective-permute-done((bf16[16,256,256]{2,1,0:T(8,128)(2,1)S(1)}, bf16[16,256,256]{2,1,0:T(8,128)(2,1)S(1)}, u32[]{:S(2)}, u32[]{:S(2)}) %collective-permute-start.1) | collective-permute-done | bytes 2097184 | tf_op jit(solution)/shard_map/ppermute | solution.py:12
  61.3 2.8 collective-permute-start.2
  64.2 23.5 %collective-permute-done.2 = bf16[16,256,256]{2,1,0:T(8,128)(2,1)} collective-permute-done((bf16[16,256,256]{2,1,0:T(8,128)(2,1)S(1)}, bf16[16,256,256]{2,1,0:T(8,128)(2,1)}, u32[]{:S(2)}, u32[]{:S(2)}) %collective-permute-start.2) | collective-permute-done | bytes 2097184 | tf_op jit(solution)/shard_map/ppermute | solution.py:12
  87.7 3.2 collective-permute-start.3
  90.9 23.9 %collective-permute-done.3 = bf16[16,256,256]{2,1,0:T(8,128)(2,1)S(1)} collective-permute-done((bf16[16,256,256]{2,1,0:T(8,128)(2,1)}, bf16[16,256,256]{2,1,0:T(8,128)(2,1)S(1)}, u32[]{:S(2)}, u32[]{:S(2)}) %collective-permute-start.3) | collective-permute-done | bytes 2097184 | tf_op jit(solution)/shard_map/ppermute | solution.py:12
  116.1 3.1 collective-permute-start.4
  119.2 23.6 %collective-permute-done.4 = bf16[16,256,256]{2,1,0:T(8,128)(2,1)S(1)} collective-permute-done((bf16[16,256,256]{2,1,0:T(8,128)(2,1)S(1)}, bf16[16,256,256]{2,1,0:T(8,128)(2,1)S(1)}, u32[]{:S(2)}, u32[]{:S(2)}) %collective-permute-start.4) | collective-permute-done | bytes 2097184 | tf_op jit(solution)/shard_map/ppermute | solution.py:12
  144.1 3.2 collective-permute-start.5
  147.3 23.6 %collective-permute-done.5 = bf16[16,256,256]{2,1,0:T(8,128)(2,1)} collective-permute-done((bf16[16,256,256]{2,1,0:T(8,128)(2,1)S(1)}, bf16[16,256,256]{2,1,0:T(8,128)(2,1)}, u32[]{:S(2)}, u32[]{:S(2)}) %collective-permute-start.5) | collective-permute-done | bytes 2097184 | tf_op jit(solution)/shard_map/ppermute | solution.py:12
  170.9 3.2 collective-permute-start.6
  174.1 50.4 %copy.8 = bf16[512,128,256,1]{0,1,2,3:T(8,128)(2,1)} copy(bf16[512,128,256,1]{2,1,0,3:T(8,128)(2,1)} %bitcast.19) | data formatting | bytes 67108864 | tf_op args[2]
  224.8 2.0 constant_dynamic-update-slice_fusion.14
  226.9 2.0 constant_dynamic-update-slice_fusion.13
  234.6 1.9 constant_dynamic-update-slice_fusion.9
  243.4 1.9 constant_dynamic-update-slice_fusion.1
  247.2 6.6 %constant_dynamic-slice_fusion = bf16[16,256,2048]{2,1,0:T(8,128)(2,1)} fusion(bf16[16,256,4096]{2,1,0:T(8,128)(2,1)S(1)} %constant_dynamic-update-slice_fusion, s32[]{:T(128)S(6)} %select_n.14), kind=kLoop, calls=%fused_computation.17 | loop fusion | bytes 33554436 | tf_op jit(solution)/shard_map/jit(_roll_dynamic)/dynamic_slice | solution.py:15
  253.8 42.0 %convert_bitcast_fusion = bf16[512,8,16,128]{3,1,2,0:T(8,128)(2,1)} fusion(bf16[4096,2048]{1,0:T(8,128)(2,1)} %bitcast.20, bf16[2048,2048]{1,0:T(8,128)(2,1)} %bitcast.23), kind=kOutput, calls=%fused_computation | convolution fusion | flops 34368126976 | bytes 41943040 | tf_op jit(solution)/shard_map/dot_general | solution.py:26
  295.8 9.6 %copy.12 = bf16[512,8,16,128]{3,2,1,0:T(8,128)(2,1)S(1)} copy(bf16[512,8,16,128]{3,1,2,0:T(8,128)(2,1)} %convert_bitcast_fusion) | data formatting | bytes 33554432
  305.5 22.5 %fusion = f32[16,16,512,1]{2,0,3,1:T(8,128)S(1)} fusion(bf16[16,128,16,256]{1,0,3,2:T(8,128)(2,1)S(1)} %bitcast.21, bf16[512,128,256,1]{0,1,2,3:T(8,128)(2,1)} %copy.8), kind=kOutput, calls=%fused_computation.18 | convolution fusion | flops 8589934592 | bytes 50855936 | tf_op jit(solution)/shard_map/acbd,pcd->pab/dot_general | solution.py:30
  329.4 33.6 %reduce-scatter.3.cloned.1.call-done = f32[64,256]{1,0:T(8,128)} async-done(((f32[512,256]{1,0:T(8,128)}), f32[64,256]{1,0:T(8,128)}) %reduce-scatter.3.cloned.1.call-update) | async-done | bytes 65552 | tf_op jit(solution)/shard_map/reduce_scatter | solution.py:34
  363.0 21.6 %reduce-scatter.5.cloned.1.call-done = f32[16,256]{1,0:T(8,128)} async-done(((f32[64,256]{1,0:T(8,128)}), f32[16,256]{1,0:T(8,128)}) %reduce-scatter.5.cloned.1.call-update) | async-done | bytes 16400 | tf_op jit(solution)/shard_map/reduce_scatter | solution.py:35
  (38 shorter events, 20.1 us)
Async XLA Ops:
  6.5 247.3 %all-gather.2.cloned.1.call-start = ((), (), s32[]{:S(2)}) async-start(), calls=%async_computation.2 | async-start | bytes 10485760 | tf_op jit(solution)/shard_map/all_gather | solution.py:22
  6.5 27.2 %collective-permute-start = (bf16[16,256,256]{2,1,0:T(8,128)(2,1)}, bf16[16,256,256]{2,1,0:T(8,128)(2,1)S(1)}, u32[]{:S(2)}, u32[]{:S(2)}) collective-permute-start(bf16[16,256,256]{2,1,0:T(8,128)(2,1)} %param.4), channel_id=1, source_target_pairs={{0,28},{4,0},{8,4},{12,8},{16,12},{20,16},{24,20},{28,24},{1,29},{... | collective-permute-start | bytes 6291464 | tf_op jit(solution)/shard_map/ppermute | solution.py:12
  33.8 1.3 copy-start.1
  35.1 26.3 %collective-permute-start.1 = (bf16[16,256,256]{2,1,0:T(8,128)(2,1)S(1)}, bf16[16,256,256]{2,1,0:T(8,128)(2,1)S(1)}, u32[]{:S(2)}, u32[]{:S(2)}) collective-permute-start(bf16[16,256,256]{2,1,0:T(8,128)(2,1)S(1)} %collective-permute-done), channel_id=1, source_target_pairs={{0,28},{4,0},{8,4},{12,8},{16,12},{20,16},{24,20},{28,24},{1,29},{... | collective-permute-start | bytes 6291464 | tf_op jit(solution)/shard_map/ppermute | solution.py:12
  61.3 112.8 %copy-start.3 = (bf16[16,256,256]{2,1,0:T(8,128)(2,1)}, bf16[16,256,256]{2,1,0:T(8,128)(2,1)S(1)}, u32[]{:S(2)}) copy-start(bf16[16,256,256]{2,1,0:T(8,128)(2,1)S(1)} %collective-permute-done.1) | copy-start | bytes 6291460
  61.3 26.4 %collective-permute-start.2 = (bf16[16,256,256]{2,1,0:T(8,128)(2,1)S(1)}, bf16[16,256,256]{2,1,0:T(8,128)(2,1)}, u32[]{:S(2)}, u32[]{:S(2)}) collective-permute-start(bf16[16,256,256]{2,1,0:T(8,128)(2,1)S(1)} %collective-permute-done.1), channel_id=1, source_target_pairs={{0,28},{4,0},{8,4},{12,8},{16,12},{20,16},{24,20},{28,24},{1,29},{... | collective-permute-start | bytes 6291464 | tf_op jit(solution)/shard_map/ppermute | solution.py:12
  64.2 298.8 %reduce-scatter.3.cloned.1.call-start = ((), (), s32[]{:S(2)}) async-start(), calls=%async_computation.3 | async-start | bytes 589824 | tf_op jit(solution)/shard_map/reduce_scatter | solution.py:34
  87.7 27.1 %collective-permute-start.3 = (bf16[16,256,256]{2,1,0:T(8,128)(2,1)}, bf16[16,256,256]{2,1,0:T(8,128)(2,1)S(1)}, u32[]{:S(2)}, u32[]{:S(2)}) collective-permute-start(bf16[16,256,256]{2,1,0:T(8,128)(2,1)} %collective-permute-done.2), channel_id=1, source_target_pairs={{0,28},{4,0},{8,4},{12,8},{16,12},{20,16},{24,20},{28,24},{1,29},{... | collective-permute-start | bytes 6291464 | tf_op jit(solution)/shard_map/ppermute | solution.py:12
  114.8 1.3 copy-start.5
  116.1 26.7 %collective-permute-start.4 = (bf16[16,256,256]{2,1,0:T(8,128)(2,1)S(1)}, bf16[16,256,256]{2,1,0:T(8,128)(2,1)S(1)}, u32[]{:S(2)}, u32[]{:S(2)}) collective-permute-start(bf16[16,256,256]{2,1,0:T(8,128)(2,1)S(1)} %collective-permute-done.3), channel_id=1, source_target_pairs={{0,28},{4,0},{8,4},{12,8},{16,12},{20,16},{24,20},{28,24},{1,29},{... | collective-permute-start | bytes 6291464 | tf_op jit(solution)/shard_map/ppermute | solution.py:12
  142.8 1.4 copy-start.7
  144.1 26.8 %collective-permute-start.5 = (bf16[16,256,256]{2,1,0:T(8,128)(2,1)S(1)}, bf16[16,256,256]{2,1,0:T(8,128)(2,1)}, u32[]{:S(2)}, u32[]{:S(2)}) collective-permute-start(bf16[16,256,256]{2,1,0:T(8,128)(2,1)S(1)} %collective-permute-done.4), channel_id=1, source_target_pairs={{0,28},{4,0},{8,4},{12,8},{16,12},{20,16},{24,20},{28,24},{1,29},{... | collective-permute-start | bytes 6291464 | tf_op jit(solution)/shard_map/ppermute | solution.py:12
  170.9 65.6 %collective-permute-start.6 = (bf16[16,256,256]{2,1,0:T(8,128)(2,1)}, bf16[16,256,256]{2,1,0:T(8,128)(2,1)}, u32[]{:S(2)}, u32[]{:S(2)}) collective-permute-start(bf16[16,256,256]{2,1,0:T(8,128)(2,1)} %collective-permute-done.5), channel_id=1, source_target_pairs={{0,28},{4,0},{8,4},{12,8},{16,12},{20,16},{24,20},{28,24},{1,29},{... | collective-permute-start | bytes 6291464 | tf_op jit(solution)/shard_map/ppermute | solution.py:12
  174.1 50.4 %copy-start = (bf16[16,256,256]{2,1,0:T(8,128)(2,1)S(1)}, bf16[16,256,256]{2,1,0:T(8,128)(2,1)}, u32[]{:S(2)}) copy-start(bf16[16,256,256]{2,1,0:T(8,128)(2,1)} %param.4) | copy-start | bytes 6291460
  224.5 14.1 %copy-start.2 = (bf16[16,256,256]{2,1,0:T(8,128)(2,1)S(1)}, bf16[16,256,256]{2,1,0:T(8,128)(2,1)}, u32[]{:S(2)}) copy-start(bf16[16,256,256]{2,1,0:T(8,128)(2,1)} %copy-done.1) | copy-start | bytes 6291460
  224.5 14.5 %copy-start.4 = (bf16[16,256,256]{2,1,0:T(8,128)(2,1)S(1)}, bf16[16,256,256]{2,1,0:T(8,128)(2,1)}, u32[]{:S(2)}) copy-start(bf16[16,256,256]{2,1,0:T(8,128)(2,1)} %copy-done.3) | copy-start | bytes 6291460
  224.5 16.7 %copy-start.6 = (bf16[16,256,256]{2,1,0:T(8,128)(2,1)S(1)}, bf16[16,256,256]{2,1,0:T(8,128)(2,1)}, u32[]{:S(2)}) copy-start(bf16[16,256,256]{2,1,0:T(8,128)(2,1)} %copy-done.5) | copy-start | bytes 6291460
  329.3 55.2 %reduce-scatter.5.cloned.1.call-start = ((), (), s32[]{:S(2)}) async-start(), calls=%async_computation.4 | async-start | bytes 81920 | tf_op jit(solution)/shard_map/reduce_scatter | solution.py:35
Sparse Core Ops, SparseCore 0:
  64.3 148.9 all-gather.1
  329.4 33.5 reduce-scatter.2
  365.2 19.2 reduce-scatter.4
